TPU v7x, 32 devices: a whole 2x2x4 slice. The times are simulated.
32 devices in a mesh: space: 16 (over z, y, core), filt: 2 (over x).
Axes of the slice: x: 2, y: 2, z: 4, core: 2. Of those that a mesh axis runs over, the one named last changes fastest.
Arguments:
- volume: bfloat16 [64, 32, 4, 256], P(None, 'space', 'filt'), may hold values from -6 to 6
- first_weight: bfloat16 [27, 64, 64], replicated, may hold values from -0.15625 to 0.15625
- second_weight: bfloat16 [27, 128, 64], P(None, 'filt'), may hold values from -0.15625 to 0.15625
- cotangent: bfloat16 [128, 16, 2, 128], P('filt', 'space'), may hold values from -24 to 24
Outputs:
- features: bfloat16 [128, 16, 2, 128], P('filt', 'space')
- volume_grad: bfloat16 [64, 32, 4, 256], P(None, 'space', 'filt')
- first_grad: float32 [27, 64, 64], replicated
- second_grad: float32 [27, 128, 64], P(None, 'filt')
All inputs are finite; a program needn't handle non-finite values.
Results may differ from a plain program's by a relative error of at most 0.019.
Values may be sent and summed in bfloat16 or wider, within the bound.
No kernel may reach another device: no remote copies, remote signals or barrier semaphores. Data moves between devices by JAX's collectives and lax.ppermute only.
A program may use at most 64 MiB of HBM per device.

v0:
```python
import jax
import jax.numpy as jnp
from jax import lax
from jax.sharding import PartitionSpec as P


def extended(cells, sides, width):
    for axis, dim in sides:
        count = lax.axis_size(axis)
        ends = count - 1
        head = lax.slice_in_dim(cells, 0, width, axis=dim)
        tail = lax.slice_in_dim(cells, cells.shape[dim] - width, cells.shape[dim], axis=dim)
        cells = jnp.concatenate(
            [
                lax.ppermute(tail, axis, [(i, (i + 1) % count) for i in range(ends)]),
                cells,
                lax.ppermute(head, axis, [((i + 1) % count, i) for i in range(ends)]),
            ],
            axis=dim,
        )
    return cells


def silu_slope(values):
    sigmoid_part = jax.nn.sigmoid(values)
    return sigmoid_part * (1.0 + values * (1.0 - sigmoid_part))


def pad_depth(volume_field):
    return jnp.pad(volume_field, ((0, 0), (0, 0), (0, 0), (1, 1)))


def window(padded, offset_x, offset_y, offset_z, extents):
    extent_x, extent_y, extent_z = extents
    section = lax.slice(
        padded,
        (0, offset_x, offset_y, offset_z),
        (padded.shape[0], offset_x + extent_x, offset_y + extent_y, offset_z + extent_z),
    )
    return section.reshape(padded.shape[0], extent_x * extent_y * extent_z)


def conv_forward(padded, weight, extents):
    outputs, inputs = (weight.shape[1], weight.shape[2])
    running = jnp.zeros((outputs, extents[0] * extents[1] * extents[2]), jnp.float32)
    for offset_x in range(3):
        for offset_y in range(3):
            tap_base = offset_x * 9 + offset_y * 3
            stacked = jnp.concatenate(
                [window(padded, offset_x, offset_y, offset_z, extents) for offset_z in range(3)],
                axis=0,
            )
            matrices = jnp.transpose(weight[tap_base : tap_base + 3], (1, 0, 2)).reshape(
                outputs, 3 * inputs
            )
            running = running + jnp.dot(matrices, stacked, preferred_element_type=jnp.float32)
    return running


def conv_transpose(padded, weight, extents):
    outputs, inputs = (weight.shape[1], weight.shape[2])
    running = jnp.zeros((inputs, extents[0] * extents[1] * extents[2]), jnp.float32)
    for offset_x in range(3):
        for offset_y in range(3):
            tap_base = offset_x * 9 + offset_y * 3
            stacked = jnp.concatenate(
                [window(padded, offset_x, offset_y, offset_z, extents) for offset_z in range(3)],
                axis=0,
            )
            tap_block = weight[24 - tap_base : 27 - tap_base][::-1]
            matrices = jnp.transpose(tap_block, (2, 0, 1)).reshape(inputs, 3 * outputs)
            running = running + jnp.dot(matrices, stacked, preferred_element_type=jnp.float32)
    return running


def conv_weights(grad_rows, padded, extents):
    outputs, inputs = (grad_rows.shape[0], padded.shape[0])
    blocks = []
    for offset_x in range(3):
        for offset_y in range(3):
            stacked = jnp.concatenate(
                [window(padded, offset_x, offset_y, offset_z, extents) for offset_z in range(3)],
                axis=0,
            )
            section = lax.dot_general(
                grad_rows, stacked, (((1,), (1,)), ((), ())), preferred_element_type=jnp.float32
            )
            blocks.append(jnp.transpose(section.reshape(outputs, 3, inputs), (1, 0, 2)))
    return jnp.concatenate(blocks, axis=0)


def pool_cells(hidden):
    channels, size_x, size_y, size_z = hidden.shape
    pair_table = (jnp.arange(size_z)[:, None] // 2 == jnp.arange(size_z // 2)[None, :]).astype(
        jnp.bfloat16
    )
    depth_sums = jnp.dot(hidden.reshape(-1, size_z), pair_table, preferred_element_type=jnp.float32)
    depth_sums = depth_sums.reshape(channels, size_x // 2, 2, size_y // 2, 2, size_z // 2)
    return (0.125 * depth_sums.sum(axis=(2, 4))).astype(jnp.bfloat16)


def spread_cells(grad_field):
    scaled = 0.125 * grad_field
    scaled = jnp.repeat(scaled, 2, axis=1)
    scaled = jnp.repeat(scaled, 2, axis=2)
    return jnp.repeat(scaled, 2, axis=3)


def local(volume, first_weight, second_weight, cotangent):
    count_space = lax.axis_size("space")
    count_filt = lax.axis_size("filt")
    channels = volume.shape[0]
    fine_shape = volume.shape[1:]
    fine_cells = fine_shape[0] * fine_shape[1] * fine_shape[2] * count_space * count_filt
    fine_scale = 1.0 / fine_cells**0.5
    padded_in = pad_depth(extended(volume, (("space", 1), ("filt", 2)), 1))
    first_pre = conv_forward(padded_in, first_weight, fine_shape)
    hidden = jax.nn.silu(first_pre).astype(jnp.bfloat16).reshape((channels,) + fine_shape)
    pooled = pool_cells(hidden)
    brick_shape = pooled.shape[1:]
    brick_cells = brick_shape[0] * brick_shape[1] * brick_shape[2]
    bottom_scale = 1.0 / (brick_cells * count_space * count_filt) ** 0.5
    filters = second_weight.shape[1]
    whole_weight = lax.all_gather(second_weight, "filt", axis=1, tiled=True)
    total_filters = whole_weight.shape[1]
    padded_pool = pad_depth(extended(pooled, (("space", 1), ("filt", 2)), 1))
    second_pre = conv_forward(padded_pool, whole_weight, brick_shape)
    local_out = jax.nn.silu(second_pre).astype(jnp.bfloat16).reshape((total_filters,) + brick_shape)
    features = lax.all_to_all(local_out, "filt", split_axis=0, concat_axis=2, tiled=True)
    local_cot = lax.all_to_all(cotangent, "filt", split_axis=2, concat_axis=0, tiled=True)
    down_grad = (
        local_cot.reshape(total_filters, -1).astype(jnp.float32) * silu_slope(second_pre)
    ).astype(jnp.bfloat16)
    summed = lax.psum(conv_weights(down_grad, padded_pool, brick_shape), ("space", "filt"))
    second_grad = (
        lax.dynamic_slice_in_dim(summed, lax.axis_index("filt") * filters, filters, 1)
        * bottom_scale
    )
    padded_down = pad_depth(
        extended(down_grad.reshape((total_filters,) + brick_shape), (("space", 1), ("filt", 2)), 1)
    )

    def add_group(group_index, running):
        group_rows = lax.dynamic_slice_in_dim(padded_down, group_index * filters, filters, 0)
        tap_block = lax.dynamic_slice_in_dim(whole_weight, group_index * filters, filters, 1)
        section = conv_transpose(group_rows, tap_block, brick_shape)
        return running + lax.optimization_barrier(section.astype(jnp.bfloat16)).astype(jnp.float32)

    pool_grad = lax.fori_loop(
        0, count_filt, add_group, jnp.zeros((channels, brick_cells), jnp.float32)
    )
    hidden_grad = spread_cells(pool_grad.reshape((channels,) + brick_shape))
    first_down = (hidden_grad.reshape(channels, -1) * silu_slope(first_pre)).astype(jnp.bfloat16)
    first_grad = (
        lax.psum(conv_weights(first_down, padded_in, fine_shape), ("space", "filt")) * fine_scale
    )
    padded_back = pad_depth(
        extended(first_down.reshape((channels,) + fine_shape), (("space", 1), ("filt", 2)), 1)
    )
    volume_grad = (
        conv_transpose(padded_back, first_weight, fine_shape)
        .astype(jnp.bfloat16)
        .reshape((channels,) + fine_shape)
    )
    return (features, volume_grad, first_grad, second_grad)


def solution(mesh):
    placed = (
        P(None, "space", "filt", None),
        P(),
        P(None, "filt", None),
        P("filt", "space", None, None),
    )
    return jax.shard_map(
        local,
        mesh=mesh,
        in_specs=placed,
        out_specs=(
            P("filt", "space", None, None),
            P(None, "space", "filt", None),
            P(),
            P(None, "filt", None),
        ),
        check_vma=False,
    )
```

profile of v0, /device:TPU:0, one launch (start us, length us, event | category | flops | bytes accessed | tf_op | source)
XLA Modules:
  0.0 316.7 jit_solution(11860188222224926915)
XLA Ops:
  7.2 1.4 copy.107
  8.5 4.2 %all-to-all-start.1 = ((bf16[64,1,2,128]{3,0,1,2:T(8,128)(2,1)}), bf16[64,1,2,128]{3,0,1,2:T(8,128)(2,1)}, u32[]{:S(2)}, u32[]{:S(2)}) async-start(bf16[64,1,2,128]{3,0,1,2:T(8,128)(2,1)} %copy.107), calls=%async_computation.1 | async-start | bytes 65536 | tf_op jit(solution)/shard_map/all_to_all | solution.py:130
  12.8 1.0 fusion.162
  13.7 1.3 collective-permute-start.1
  15.0 3.0 collective-permute-start
  18.1 1.3 copy.96
  19.4 15.2 %all_gather.3 = bf16[27,128,64]{2,0,1:T(8,128)(2,1)S(1)} all-gather(bf16[27,64,64]{2,0,1:T(8,128)(2,1)S(1)} %copy.96), channel_id=1, replica_groups=mesh['space'=16,'filt'=2] {'filt'}, dimensions={1}, use_global_device_ids=true | all-gather | bytes 663552 | tf_op jit(solution)/shard_map/all_gather | solution.py:124
  34.6 1.3 fusion.155
  36.4 1.2 fusion.160
  37.6 4.2 %collective-permute-start.2 = (bf16[64,4,1,256]{3,2,1,0:T(2,128)(2,1)}, bf16[64,4,1,256]{3,2,1,0:T(2,128)(2,1)S(1)}, u32[]{:S(2)}, u32[]{:S(2)}) collective-permute-start(bf16[64,4,1,256]{3,2,1,0:T(2,128)(2,1)} %get-tuple-element.266), channel_id=1, source_target_pairs={{0,1},{2,3},{4,5},{6,7},{8,9},{10,11},{12,13},{14,15},{16,17},{18,... | collective-permute-start | bytes 393224 | tf_op jit(solution)/shard_map/ppermute | solution.py:15
  41.8 1.5 collective-permute-start.3
  43.3 1.0 fusion.158
  45.5 1.8 copy.153
  47.3 1.0 copy.152
  48.3 1.6 copy.151
  50.0 1.6 copy.150
  51.6 1.6 copy.149
  56.1 1.4 rev.98
  70.2 1.7 pad_maximum_fusion.9
  75.6 2.4 select_maximum_fusion.2
  78.1 2.9 fusion.157
  86.4 1.0 constant_dynamic-update-slice_fusion.11
  87.3 0.9 constant_dynamic-update-slice_fusion.14
  91.8 0.9 multiply_convert_fusion.1
  93.1 1.3 collective-permute-start.5
  94.4 3.0 collective-permute-start.4
  97.5 0.8 bitcast_convert_fusion
  98.4 1.3 collective-permute-start.7
  99.7 4.8 %collective-permute-start.6 = (bf16[64,3,1,128]{3,0,2,1:T(8,128)(2,1)S(1)}, bf16[64,3,1,128]{3,0,2,1:T(8,128)(2,1)S(1)}, u32[]{:S(2)}, u32[]{:S(2)}) collective-permute-start(bf16[64,3,1,128]{3,0,2,1:T(8,128)(2,1)S(1)} %pad_maximum_fusion.18), channel_id=1, source_target_pairs={{0,1},{2,3},{4,5},{6,7},{8,9},{10,11},{12,13},{14,15},{16,17},{18,... | collective-permute-start | bytes 147464 | tf_op jit(solution)/shard_map/ppermute | solution.py:15
  104.5 1.5 collective-permute-done.6
  108.2 1.3 collective-permute-start.9
  109.5 3.3 %collective-permute-start.8 = (bf16[128,1,1,128]{0,3,2,1:T(8,128)(2,1)S(1)}, bf16[128,1,1,128]{0,3,2,1:T(8,128)(2,1)S(1)}, u32[]{:S(2)}, u32[]{:S(2)}) collective-permute-start(bf16[128,1,1,128]{0,3,2,1:T(8,128)(2,1)S(1)} %bitcast.409), channel_id=1, source_target_pairs={{0,2},{2,4},{4,6},{6,8},{8,10},{10,12},{12,14},{14,16},{16,18},{18... | collective-permute-start | bytes 98312 | tf_op jit(solution)/shard_map/ppermute | solution.py:15
  115.9 3.3 %all-to-all-start = ((bf16[2,2,4096]{2,1,0:T(2,128)(2,1)}), bf16[2,2,4096]{2,1,0:T(2,128)(2,1)S(1)}, u32[]{:S(2)}, u32[]{:S(2)}) async-start(bf16[2,2,4096]{2,1,0:T(2,128)(2,1)} %reshape.942), calls=%async_computation | async-start | bytes 65536 | tf_op jit(solution)/shard_map/all_to_all | solution.py:129
  119.6 0.8 copy.127
  120.4 0.8 copy.126
  121.2 0.8 copy.125
  122.1 0.8 copy.124
  122.9 0.8 copy.123
  123.7 0.9 bitcast_dynamic-update-slice_fusion.8
  124.6 0.9 bitcast_dynamic-update-slice_fusion.7
  125.6 0.9 bitcast_dynamic-update-slice_fusion.6
  126.5 0.9 bitcast_dynamic-update-slice_fusion.5
  127.5 0.9 bitcast_dynamic-update-slice_fusion.4
  128.8 1.3 collective-permute-start.11
  130.1 4.6 %collective-permute-start.10 = (bf16[128,3,1,128]{0,3,2,1:T(8,128)(2,1)S(1)}, bf16[128,3,1,128]{0,3,2,1:T(8,128)(2,1)S(1)}, u32[]{:S(2)}, u32[]{:S(2)}) collective-permute-start(bf16[128,3,1,128]{0,3,2,1:T(8,128)(2,1)S(1)} %pad_maximum_fusion.17), channel_id=1, source_target_pairs={{0,1},{2,3},{4,5},{6,7},{8,9},{10,11},{12,13},{14,15},{16,17},{18,... | collective-permute-start | bytes 294920 | tf_op jit(solution)/shard_map/ppermute | solution.py:15
  134.8 0.8 copy.132
  135.6 1.3 collective-permute-done.10
  137.4 5.5 %while.14 = (s32[]{:T(128)}, f32[64,128]{1,0:T(8,128)}, bf16[27,128,64]{2,1,0:T(8,128)(2,1)S(1)}, bf16[128,3,3,130]{3,0,2,1:T(8,128)(2,1)S(1)}, s32[]{:T(128)}, ...) while((s32[]{:T(128)}, f32[64,128]{1,0:T(8,128)}, ...), condition=%wide.region_2.3_spmd.clone, body=%wide.region_1.2_spmd.clone.sunk | while | flops 29736976 | bytes 3318213 | solution.py:149
  142.9 0.9 broadcast_multiply_fusion.1
  147.0 1.3 collective-permute-start.13
  148.3 4.5 %collective-permute-start.12 = (bf16[64,1,2,256]{3,2,1,0:T(2,128)(2,1)S(1)}, bf16[64,1,2,256]{3,2,1,0:T(2,128)(2,1)S(1)}, u32[]{:S(2)}, u32[]{:S(2)}) collective-permute-start(bf16[64,1,2,256]{3,2,1,0:T(2,128)(2,1)S(1)} %get-tuple-element.272), channel_id=1, source_target_pairs={{0,2},{2,4},{4,6},{6,8},{8,10},{10,12},{12,14},{14,16},{16,18},{18... | collective-permute-start | bytes 196616 | tf_op jit(solution)/shard_map/ppermute | solution.py:15
  154.6 4.0 %collective-permute-start.14 = (bf16[64,4,1,256]{3,2,1,0:T(2,128)(2,1)S(1)}, bf16[64,4,1,256]{3,2,1,0:T(2,128)(2,1)S(1)}, u32[]{:S(2)}, u32[]{:S(2)}) collective-permute-start(bf16[64,4,1,256]{3,2,1,0:T(2,128)(2,1)S(1)} %get-tuple-element.261), channel_id=1, source_target_pairs={{0,1},{2,3},{4,5},{6,7},{8,9},{10,11},{12,13},{14,15},{16,17},{18,... | collective-permute-start | bytes 393224 | tf_op jit(solution)/shard_map/ppermute | solution.py:15
  158.6 1.6 collective-permute-start.15
  160.2 0.9 copy-done.20
  161.3 2.3 collective-permute-done.14
  163.6 4.7 %collective-permute-done.15 = bf16[64,4,1,256]{3,2,1,0:T(2,128)(2,1)S(1)} collective-permute-done((bf16[64,4,1,256]{3,2,1,0:T(2,128)(2,1)S(1)}, bf16[64,4,1,256]{3,2,1,0:T(2,128)(2,1)S(1)}, u32[]{:S(2)}, u32[]{:S(2)}) %collective-permute-start.15) | collective-permute-done | bytes 131104 | tf_op jit(solution)/shard_map/ppermute | solution.py:17
  168.3 1.7 pad_maximum_fusion.1
  172.4 2.4 select_maximum_fusion
  174.8 2.9 fusion.156
  181.8 1.2 fusion.62
  186.0 120.2 %all-reduce.7.cloned.1.call-done = (f32[27,64,64]{1,2,0:T(8,128)}, f32[27,128,64]{2,1,0:T(8,128)}) async-done(((f32[27,64,64]{1,2,0:T(8,128)}, f32[27,128,64]{2,1,0:T(8,128)}), (f32[27,64,64]{1,2,0:T(8,128)}, f32[27,128,64]{2,1,0:T(8,128)})) %all-reduce.7.cloned.1.call-update) | async-done | bytes 1327120 | tf_op jit(solution)/shard_map/psum | solution.py:155
  306.2 1.4 broadcast_multiply_fusion
  307.6 1.2 copy.133
  308.9 1.0 dynamic-slice_multiply_fusion
  (443 shorter events, 55.2 us)
Async XLA Ops:
  8.5 88.9 %all-to-all-start.1 = ((bf16[64,1,2,128]{3,0,1,2:T(8,128)(2,1)}), bf16[64,1,2,128]{3,0,1,2:T(8,128)(2,1)}, u32[]{:S(2)}, u32[]{:S(2)}) async-start(bf16[64,1,2,128]{3,0,1,2:T(8,128)(2,1)} %copy.107), calls=%async_computation.1 | async-start | bytes 65536 | tf_op jit(solution)/shard_map/all_to_all | solution.py:130
  13.7 22.2 %collective-permute-start.1 = (bf16[64,1,2,256]{3,2,1,0:T(2,128)(2,1)S(1)}, bf16[64,1,2,256]{3,2,1,0:T(2,128)(2,1)S(1)}, u32[]{:S(2)}, u32[]{:S(2)}) collective-permute-start(bf16[64,1,2,256]{3,2,1,0:T(2,128)(2,1)S(1)} %get-tuple-element.276), channel_id=1, source_target_pairs={{2,0},{4,2},{6,4},{8,6},{10,8},{12,10},{14,12},{16,14},{18,16},{20... | collective-permute-start | bytes 196616 | tf_op jit(solution)/shard_map/ppermute | solution.py:17
  15.0 20.9 %collective-permute-start = (bf16[64,1,2,256]{3,2,1,0:T(2,128)(2,1)S(1)}, bf16[64,1,2,256]{3,2,1,0:T(2,128)(2,1)S(1)}, u32[]{:S(2)}, u32[]{:S(2)}) collective-permute-start(bf16[64,1,2,256]{3,2,1,0:T(2,128)(2,1)S(1)} %get-tuple-element.277), channel_id=1, source_target_pairs={{0,2},{2,4},{4,6},{6,8},{8,10},{10,12},{12,14},{14,16},{16,18},{18... | collective-permute-start | bytes 196616 | tf_op jit(solution)/shard_map/ppermute | solution.py:15
  19.4 16.6 %copy-start.17 = (bf16[64,2,2,256]{3,2,1,0:T(2,128)(2,1)S(1)}, bf16[64,2,2,256]{3,2,1,0:T(2,128)(2,1)}, u32[]{:S(2)}) copy-start(bf16[64,2,2,256]{3,2,1,0:T(2,128)(2,1)} %param.6) | copy-start | bytes 393220
  34.6 8.6 %copy-start.35 = (bf16[27,64,64]{2,1,0:T(8,128)(2,1)S(1)}, bf16[27,64,64]{2,1,0:T(8,128)(2,1)}, u32[]{:S(2)}) copy-start(bf16[27,64,64]{2,1,0:T(8,128)(2,1)} %param.7) | copy-start | bytes 663556
  37.6 32.6 %collective-permute-start.2 = (bf16[64,4,1,256]{3,2,1,0:T(2,128)(2,1)}, bf16[64,4,1,256]{3,2,1,0:T(2,128)(2,1)S(1)}, u32[]{:S(2)}, u32[]{:S(2)}) collective-permute-start(bf16[64,4,1,256]{3,2,1,0:T(2,128)(2,1)} %get-tuple-element.266), channel_id=1, source_target_pairs={{0,1},{2,3},{4,5},{6,7},{8,9},{10,11},{12,13},{14,15},{16,17},{18,... | collective-permute-start | bytes 393224 | tf_op jit(solution)/shard_map/ppermute | solution.py:15
  41.8 28.4 %collective-permute-start.3 = (bf16[64,4,1,256]{3,2,1,0:T(2,128)(2,1)}, bf16[64,4,1,256]{3,2,1,0:T(2,128)(2,1)S(1)}, u32[]{:S(2)}, u32[]{:S(2)}) collective-permute-start(bf16[64,4,1,256]{3,2,1,0:T(2,128)(2,1)} %get-tuple-element.267), channel_id=1, source_target_pairs={{1,0},{3,2},{5,4},{7,6},{9,8},{11,10},{13,12},{15,14},{17,16},{19,... | collective-permute-start | bytes 393224 | tf_op jit(solution)/shard_map/ppermute | solution.py:17
  45.4 12.1 %copy-start.67 = (bf16[64,3,64]{2,0,1:T(8,128)(2,1)S(1)}, bf16[64,3,64]{2,0,1:T(8,128)(2,1)}, u32[]{:S(2)}) copy-start(bf16[64,3,64]{2,0,1:T(8,128)(2,1)} %get-tuple-element.223) | copy-start | bytes 73732
  45.4 12.9 %copy-start.66 = (bf16[64,3,64]{2,0,1:T(8,128)(2,1)S(1)}, bf16[64,3,64]{2,0,1:T(8,128)(2,1)}, u32[]{:S(2)}) copy-start(bf16[64,3,64]{2,0,1:T(8,128)(2,1)} %get-tuple-element.224) | copy-start | bytes 73732
  45.4 13.6 %copy-start.65 = (bf16[64,3,64]{2,0,1:T(8,128)(2,1)S(1)}, bf16[64,3,64]{2,0,1:T(8,128)(2,1)}, u32[]{:S(2)}) copy-start(bf16[64,3,64]{2,0,1:T(8,128)(2,1)} %get-tuple-element.225) | copy-start | bytes 73732
  45.4 14.3 %copy-start.64 = (bf16[64,3,64]{2,0,1:T(8,128)(2,1)S(1)}, bf16[64,3,64]{2,0,1:T(8,128)(2,1)}, u32[]{:S(2)}) copy-start(bf16[64,3,64]{2,0,1:T(8,128)(2,1)} %get-tuple-element.226) | copy-start | bytes 73732
  45.4 15.0 %copy-start.63 = (bf16[64,3,64]{2,0,1:T(8,128)(2,1)S(1)}, bf16[64,3,64]{2,0,1:T(8,128)(2,1)}, u32[]{:S(2)}) copy-start(bf16[64,3,64]{2,0,1:T(8,128)(2,1)} %get-tuple-element.227) | copy-start | bytes 73732
  45.4 15.7 %copy-start.62 = (bf16[64,3,64]{2,0,1:T(8,128)(2,1)S(1)}, bf16[64,3,64]{2,0,1:T(8,128)(2,1)}, u32[]{:S(2)}) copy-start(bf16[64,3,64]{2,0,1:T(8,128)(2,1)} %get-tuple-element.228) | copy-start | bytes 73732
  45.4 16.4 %copy-start.61 = (bf16[64,3,64]{2,0,1:T(8,128)(2,1)S(1)}, bf16[64,3,64]{2,0,1:T(8,128)(2,1)}, u32[]{:S(2)}) copy-start(bf16[64,3,64]{2,0,1:T(8,128)(2,1)} %get-tuple-element.229) | copy-start | bytes 73732
  45.4 17.1 %copy-start.60 = (bf16[64,3,64]{2,0,1:T(8,128)(2,1)S(1)}, bf16[64,3,64]{2,0,1:T(8,128)(2,1)}, u32[]{:S(2)}) copy-start(bf16[64,3,64]{2,0,1:T(8,128)(2,1)} %get-tuple-element.230) | copy-start | bytes 73732
  45.4 17.8 %copy-start.59 = (bf16[64,3,64]{2,0,1:T(8,128)(2,1)S(1)}, bf16[64,3,64]{2,0,1:T(8,128)(2,1)}, u32[]{:S(2)}) copy-start(bf16[64,3,64]{2,0,1:T(8,128)(2,1)} %get-tuple-element.231) | copy-start | bytes 73732
  45.5 18.5 %copy-start.58 = (bf16[3,64,64]{2,1,0:T(8,128)(2,1)S(1)}, bf16[3,64,64]{2,1,0:T(8,128)(2,1)}, u32[]{:S(2)}) copy-start(bf16[3,64,64]{2,1,0:T(8,128)(2,1)} %get-tuple-element.232) | copy-start | bytes 73732
  45.5 19.1 %copy-start.57 = (bf16[3,64,64]{2,1,0:T(8,128)(2,1)S(1)}, bf16[3,64,64]{2,1,0:T(8,128)(2,1)}, u32[]{:S(2)}) copy-start(bf16[3,64,64]{2,1,0:T(8,128)(2,1)} %get-tuple-element.233) | copy-start | bytes 73732
  45.5 19.7 %copy-start.56 = (bf16[3,64,64]{2,1,0:T(8,128)(2,1)S(1)}, bf16[3,64,64]{2,1,0:T(8,128)(2,1)}, u32[]{:S(2)}) copy-start(bf16[3,64,64]{2,1,0:T(8,128)(2,1)} %get-tuple-element.234) | copy-start | bytes 73732
  45.5 20.3 %copy-start.55 = (bf16[3,64,64]{2,1,0:T(8,128)(2,1)S(1)}, bf16[3,64,64]{2,1,0:T(8,128)(2,1)}, u32[]{:S(2)}) copy-start(bf16[3,64,64]{2,1,0:T(8,128)(2,1)} %get-tuple-element.235) | copy-start | bytes 73732
  45.5 20.9 %copy-start.54 = (bf16[3,64,64]{2,1,0:T(8,128)(2,1)S(1)}, bf16[3,64,64]{2,1,0:T(8,128)(2,1)}, u32[]{:S(2)}) copy-start(bf16[3,64,64]{2,1,0:T(8,128)(2,1)} %get-tuple-element.236) | copy-start | bytes 73732
  45.5 21.5 %copy-start.53 = (bf16[3,64,64]{2,1,0:T(8,128)(2,1)S(1)}, bf16[3,64,64]{2,1,0:T(8,128)(2,1)}, u32[]{:S(2)}) copy-start(bf16[3,64,64]{2,1,0:T(8,128)(2,1)} %get-tuple-element.237) | copy-start | bytes 73732
  45.5 22.1 %copy-start.52 = (bf16[3,64,64]{2,1,0:T(8,128)(2,1)S(1)}, bf16[3,64,64]{2,1,0:T(8,128)(2,1)}, u32[]{:S(2)}) copy-start(bf16[3,64,64]{2,1,0:T(8,128)(2,1)} %get-tuple-element.238) | copy-start | bytes 73732
  45.5 22.8 %copy-start.51 = (bf16[3,64,64]{2,1,0:T(8,128)(2,1)S(1)}, bf16[3,64,64]{2,1,0:T(8,128)(2,1)}, u32[]{:S(2)}) copy-start(bf16[3,64,64]{2,1,0:T(8,128)(2,1)} %get-tuple-element.239) | copy-start | bytes 73732
  84.3 3.9 %copy-start.33 = (bf16[64,1024]{1,0:T(8,128)(2,1)S(1)}, bf16[64,1024]{1,0:T(8,128)(2,1)}, u32[]{:S(2)}) copy-start(bf16[64,1024]{1,0:T(8,128)(2,1)} %reshape.794) | copy-start | bytes 393220
  84.4 3.9 %copy-start.32 = (bf16[64,1024]{1,0:T(8,128)(2,1)S(1)}, bf16[64,1024]{1,0:T(8,128)(2,1)}, u32[]{:S(2)}) copy-start(bf16[64,1024]{1,0:T(8,128)(2,1)} %reshape.798) | copy-start | bytes 393220
  85.2 3.1 copy-start.31
  91.7 14.6 %copy-start.91 = (bf16[3,128,64]{1,2,0:T(8,128)(2,1)S(1)}, bf16[3,128,64]{1,2,0:T(8,128)(2,1)}, u32[]{:S(2)}) copy-start(bf16[3,128,64]{1,2,0:T(8,128)(2,1)} %copy.145) | copy-start | bytes 147460
  91.7 14.7 %copy-start.42 = (bf16[3,128,64]{1,2,0:T(8,128)(2,1)S(1)}, bf16[3,128,64]{1,2,0:T(8,128)(2,1)}, u32[]{:S(2)}) copy-start(bf16[3,128,64]{1,2,0:T(8,128)(2,1)} %copy.146) | copy-start | bytes 147460
  91.7 15.0 %copy-start.41 = (bf16[3,128,64]{1,2,0:T(8,128)(2,1)S(1)}, bf16[3,128,64]{1,2,0:T(8,128)(2,1)}, u32[]{:S(2)}) copy-start(bf16[3,128,64]{1,2,0:T(8,128)(2,1)} %copy.147) | copy-start | bytes 147460
  92.7 14.2 %copy-start.40 = (bf16[3,128,64]{1,2,0:T(8,128)(2,1)S(1)}, bf16[3,128,64]{1,2,0:T(8,128)(2,1)}, u32[]{:S(2)}) copy-start(bf16[3,128,64]{1,2,0:T(8,128)(2,1)} %copy.148) | copy-start | bytes 147460
  92.7 14.4 %copy-start.39 = (bf16[3,128,64]{1,2,0:T(8,128)(2,1)S(1)}, bf16[3,128,64]{1,2,0:T(8,128)(2,1)}, u32[]{:S(2)}) copy-start(bf16[3,128,64]{1,2,0:T(8,128)(2,1)} %copy.149) | copy-start | bytes 147460
  92.7 14.6 %copy-start.38 = (bf16[3,128,64]{1,2,0:T(8,128)(2,1)S(1)}, bf16[3,128,64]{1,2,0:T(8,128)(2,1)}, u32[]{:S(2)}) copy-start(bf16[3,128,64]{1,2,0:T(8,128)(2,1)} %copy.150) | copy-start | bytes 147460
  92.7 14.8 %copy-start.37 = (bf16[3,128,64]{1,2,0:T(8,128)(2,1)S(1)}, bf16[3,128,64]{1,2,0:T(8,128)(2,1)}, u32[]{:S(2)}) copy-start(bf16[3,128,64]{1,2,0:T(8,128)(2,1)} %copy.151) | copy-start | bytes 147460
  93.1 14.8 %copy-start.90 = (bf16[3,128,64]{1,2,0:T(8,128)(2,1)S(1)}, bf16[3,128,64]{1,2,0:T(8,128)(2,1)}, u32[]{:S(2)}) copy-start(bf16[3,128,64]{1,2,0:T(8,128)(2,1)} %copy.153) | copy-start | bytes 147460
  93.1 5.2 %collective-permute-start.5 = (bf16[64,1,1,128]{3,0,2,1:T(8,128)(2,1)S(1)}, bf16[64,1,1,128]{3,0,2,1:T(8,128)(2,1)S(1)}, u32[]{:S(2)}, u32[]{:S(2)}) collective-permute-start(bf16[64,1,1,128]{3,0,2,1:T(8,128)(2,1)S(1)} %fusion.245), channel_id=1, source_target_pairs={{2,0},{4,2},{6,4},{8,6},{10,8},{12,10},{14,12},{16,14},{18,16},{20... | collective-permute-start | bytes 49160 | tf_op jit(solution)/shard_map/ppermute | solution.py:17
  94.4 3.9 %collective-permute-start.4 = (bf16[64,1,1,128]{3,0,2,1:T(8,128)(2,1)S(1)}, bf16[64,1,1,128]{3,0,2,1:T(8,128)(2,1)S(1)}, u32[]{:S(2)}, u32[]{:S(2)}) collective-permute-start(bf16[64,1,1,128]{3,0,2,1:T(8,128)(2,1)S(1)} %fusion.245), channel_id=1, source_target_pairs={{0,2},{2,4},{4,6},{6,8},{8,10},{10,12},{12,14},{14,16},{16,18},{18... | collective-permute-start | bytes 49160 | tf_op jit(solution)/shard_map/ppermute | solution.py:15
  98.4 6.1 %collective-permute-start.7 = (bf16[64,3,1,128]{3,0,2,1:T(8,128)(2,1)S(1)}, bf16[64,3,1,128]{3,0,2,1:T(8,128)(2,1)S(1)}, u32[]{:S(2)}, u32[]{:S(2)}) collective-permute-start(bf16[64,3,1,128]{3,0,2,1:T(8,128)(2,1)S(1)} %pad_maximum_fusion.18), channel_id=1, source_target_pairs={{1,0},{3,2},{5,4},{7,6},{9,8},{11,10},{13,12},{15,14},{17,16},{19,... | collective-permute-start | bytes 147464 | tf_op jit(solution)/shard_map/ppermute | solution.py:17
  99.7 6.3 %collective-permute-start.6 = (bf16[64,3,1,128]{3,0,2,1:T(8,128)(2,1)S(1)}, bf16[64,3,1,128]{3,0,2,1:T(8,128)(2,1)S(1)}, u32[]{:S(2)}, u32[]{:S(2)}) collective-permute-start(bf16[64,3,1,128]{3,0,2,1:T(8,128)(2,1)S(1)} %pad_maximum_fusion.18), channel_id=1, source_target_pairs={{0,1},{2,3},{4,5},{6,7},{8,9},{10,11},{12,13},{14,15},{16,17},{18,... | collective-permute-start | bytes 147464 | tf_op jit(solution)/shard_map/ppermute | solution.py:15
  106.2 3.2 %copy-start.74 = (bf16[64,128]{1,0:T(8,128)(2,1)}, bf16[64,128]{1,0:T(8,128)(2,1)S(1)}, u32[]{:S(2)}) copy-start(bf16[64,128]{1,0:T(8,128)(2,1)S(1)} %get-tuple-element.240) | copy-start | bytes 49156
  106.3 3.2 %copy-start.76 = (bf16[64,128]{1,0:T(8,128)(2,1)}, bf16[64,128]{1,0:T(8,128)(2,1)S(1)}, u32[]{:S(2)}) copy-start(bf16[64,128]{1,0:T(8,128)(2,1)S(1)} %get-tuple-element.257) | copy-start | bytes 49156
  106.7 8.5 %copy-start.78 = (bf16[64,128]{1,0:T(8,128)(2,1)}, bf16[64,128]{1,0:T(8,128)(2,1)S(1)}, u32[]{:S(2)}) copy-start(bf16[64,128]{1,0:T(8,128)(2,1)S(1)} %get-tuple-element.280) | copy-start | bytes 49156
  108.2 20.6 %collective-permute-start.9 = (bf16[128,1,1,128]{0,3,2,1:T(8,128)(2,1)S(1)}, bf16[128,1,1,128]{0,3,2,1:T(8,128)(2,1)S(1)}, u32[]{:S(2)}, u32[]{:S(2)}) collective-permute-start(bf16[128,1,1,128]{0,3,2,1:T(8,128)(2,1)S(1)} %bitcast.408), channel_id=1, source_target_pairs={{2,0},{4,2},{6,4},{8,6},{10,8},{12,10},{14,12},{16,14},{18,16},{20... | collective-permute-start | bytes 98312 | tf_op jit(solution)/shard_map/ppermute | solution.py:17
  109.5 19.3 %collective-permute-start.8 = (bf16[128,1,1,128]{0,3,2,1:T(8,128)(2,1)S(1)}, bf16[128,1,1,128]{0,3,2,1:T(8,128)(2,1)S(1)}, u32[]{:S(2)}, u32[]{:S(2)}) collective-permute-start(bf16[128,1,1,128]{0,3,2,1:T(8,128)(2,1)S(1)} %bitcast.409), channel_id=1, source_target_pairs={{0,2},{2,4},{4,6},{6,8},{8,10},{10,12},{12,14},{14,16},{16,18},{18... | collective-permute-start | bytes 98312 | tf_op jit(solution)/shard_map/ppermute | solution.py:15
  115.9 18.9 %all-to-all-start = ((bf16[2,2,4096]{2,1,0:T(2,128)(2,1)}), bf16[2,2,4096]{2,1,0:T(2,128)(2,1)S(1)}, u32[]{:S(2)}, u32[]{:S(2)}) async-start(bf16[2,2,4096]{2,1,0:T(2,128)(2,1)} %reshape.942), calls=%async_computation | async-start | bytes 65536 | tf_op jit(solution)/shard_map/all_to_all | solution.py:129
  119.2 187.0 %all-reduce.7.cloned.1.call-start = ((), (), s32[]{:S(2)}) async-start(), calls=%async_computation.2 | async-start | bytes 5308416 | tf_op jit(solution)/shard_map/psum | solution.py:155
  122.9 5.6 %copy-start.75 = (bf16[64,128]{1,0:T(8,128)(2,1)S(1)}, bf16[64,128]{1,0:T(8,128)(2,1)}, u32[]{:S(2)}) copy-start(bf16[64,128]{1,0:T(8,128)(2,1)} %copy-done.74) | copy-start | bytes 49156
  122.9 5.6 %copy-start.77 = (bf16[64,128]{1,0:T(8,128)(2,1)S(1)}, bf16[64,128]{1,0:T(8,128)(2,1)}, u32[]{:S(2)}) copy-start(bf16[64,128]{1,0:T(8,128)(2,1)} %copy-done.76) | copy-start | bytes 49156
  122.9 5.6 %copy-start.79 = (bf16[64,128]{1,0:T(8,128)(2,1)S(1)}, bf16[64,128]{1,0:T(8,128)(2,1)}, u32[]{:S(2)}) copy-start(bf16[64,128]{1,0:T(8,128)(2,1)} %copy-done.78) | copy-start | bytes 49156
  128.8 6.7 %collective-permute-start.11 = (bf16[128,3,1,128]{0,3,2,1:T(8,128)(2,1)S(1)}, bf16[128,3,1,128]{0,3,2,1:T(8,128)(2,1)S(1)}, u32[]{:S(2)}, u32[]{:S(2)}) collective-permute-start(bf16[128,3,1,128]{0,3,2,1:T(8,128)(2,1)S(1)} %pad_maximum_fusion.17), channel_id=1, source_target_pairs={{1,0},{3,2},{5,4},{7,6},{9,8},{11,10},{13,12},{15,14},{17,16},{19,... | collective-permute-start | bytes 294920 | tf_op jit(solution)/shard_map/ppermute | solution.py:17
  130.1 6.8 %collective-permute-start.10 = (bf16[128,3,1,128]{0,3,2,1:T(8,128)(2,1)S(1)}, bf16[128,3,1,128]{0,3,2,1:T(8,128)(2,1)S(1)}, u32[]{:S(2)}, u32[]{:S(2)}) collective-permute-start(bf16[128,3,1,128]{0,3,2,1:T(8,128)(2,1)S(1)} %pad_maximum_fusion.17), channel_id=1, source_target_pairs={{0,1},{2,3},{4,5},{6,7},{8,9},{10,11},{12,13},{14,15},{16,17},{18,... | collective-permute-start | bytes 294920 | tf_op jit(solution)/shard_map/ppermute | solution.py:15
  134.7 2.7 copy-start
  137.4 6.9 %copy-start.36 = (f32[64,1024]{1,0:T(8,128)S(1)}, f32[64,1024]{1,0:T(8,128)}, u32[]{:S(2)}) copy-start(f32[64,1024]{1,0:T(8,128)} %get-tuple-element.287) | copy-start | bytes 786436
  147.0 6.7 %collective-permute-start.13 = (bf16[64,1,2,256]{3,2,1,0:T(2,128)(2,1)S(1)}, bf16[64,1,2,256]{3,2,1,0:T(2,128)(2,1)S(1)}, u32[]{:S(2)}, u32[]{:S(2)}) collective-permute-start(bf16[64,1,2,256]{3,2,1,0:T(2,128)(2,1)S(1)} %get-tuple-element.271), channel_id=1, source_target_pairs={{2,0},{4,2},{6,4},{8,6},{10,8},{12,10},{14,12},{16,14},{18,16},{20... | collective-permute-start | bytes 196616 | tf_op jit(solution)/shard_map/ppermute | solution.py:17
  148.3 5.4 %collective-permute-start.12 = (bf16[64,1,2,256]{3,2,1,0:T(2,128)(2,1)S(1)}, bf16[64,1,2,256]{3,2,1,0:T(2,128)(2,1)S(1)}, u32[]{:S(2)}, u32[]{:S(2)}) collective-permute-start(bf16[64,1,2,256]{3,2,1,0:T(2,128)(2,1)S(1)} %get-tuple-element.272), channel_id=1, source_target_pairs={{0,2},{2,4},{4,6},{6,8},{8,10},{10,12},{12,14},{14,16},{16,18},{18... | collective-permute-start | bytes 196616 | tf_op jit(solution)/shard_map/ppermute | solution.py:15
  154.6 9.0 %collective-permute-start.14 = (bf16[64,4,1,256]{3,2,1,0:T(2,128)(2,1)S(1)}, bf16[64,4,1,256]{3,2,1,0:T(2,128)(2,1)S(1)}, u32[]{:S(2)}, u32[]{:S(2)}) collective-permute-start(bf16[64,4,1,256]{3,2,1,0:T(2,128)(2,1)S(1)} %get-tuple-element.261), channel_id=1, source_target_pairs={{0,1},{2,3},{4,5},{6,7},{8,9},{10,11},{12,13},{14,15},{16,17},{18,... | collective-permute-start | bytes 393224 | tf_op jit(solution)/shard_map/ppermute | solution.py:15
  158.6 9.7 %collective-permute-start.15 = (bf16[64,4,1,256]{3,2,1,0:T(2,128)(2,1)S(1)}, bf16[64,4,1,256]{3,2,1,0:T(2,128)(2,1)S(1)}, u32[]{:S(2)}, u32[]{:S(2)}) collective-permute-start(bf16[64,4,1,256]{3,2,1,0:T(2,128)(2,1)S(1)} %get-tuple-element.262), channel_id=1, source_target_pairs={{1,0},{3,2},{5,4},{7,6},{9,8},{11,10},{13,12},{15,14},{17,16},{19,... | collective-permute-start | bytes 393224 | tf_op jit(solution)/shard_map/ppermute | solution.py:17
  178.1 3.7 %copy-start.70 = (bf16[64,1024]{1,0:T(8,128)(2,1)S(1)}, bf16[64,1024]{1,0:T(8,128)(2,1)}, u32[]{:S(2)}) copy-start(bf16[64,1024]{1,0:T(8,128)(2,1)} %reshape.850) | copy-start | bytes 393220
  178.1 3.7 %copy-start.88 = (bf16[3,64,64]{2,1,0:T(8,128)(2,1)S(1)}, bf16[3,64,64]{2,1,0:T(8,128)(2,1)}, u32[]{:S(2)}) copy-start(bf16[3,64,64]{2,1,0:T(8,128)(2,1)} %rev.90) | copy-start | bytes 73732
  179.1 3.9 %copy-start.87 = (bf16[3,64,64]{2,1,0:T(8,128)(2,1)S(1)}, bf16[3,64,64]{2,1,0:T(8,128)(2,1)}, u32[]{:S(2)}) copy-start(bf16[3,64,64]{2,1,0:T(8,128)(2,1)} %rev.91) | copy-start | bytes 73732
  179.4 3.8 %copy-start.68 = (bf16[64,1024]{1,0:T(8,128)(2,1)S(1)}, bf16[64,1024]{1,0:T(8,128)(2,1)}, u32[]{:S(2)}) copy-start(bf16[64,1024]{1,0:T(8,128)(2,1)} %reshape.858) | copy-start | bytes 393220
  179.4 3.8 %copy-start.86 = (bf16[3,64,64]{2,1,0:T(8,128)(2,1)S(1)}, bf16[3,64,64]{2,1,0:T(8,128)(2,1)}, u32[]{:S(2)}) copy-start(bf16[3,64,64]{2,1,0:T(8,128)(2,1)} %rev.92) | copy-start | bytes 73732
  180.2 2.8 copy-start.72
  306.2 2.6 copy-start.34
  (50 other events, 67.9 us)
Sparse Core Ops, SparseCore 0:
  161.2 144.9 all-reduce.6
where the time goes:
time: 318 us; the launch traced here: 317 us
  waiting for transfers between devices  131 us (41%)
  local copies, waits for them, and re-layouts  75.2 us (24%)
  starting transfers between devices  49.8 us (16%)
  between operations  16.3 us (5%)
  blocking collectives  15.2 us (5%)
  matrix products  14.6 us (5%)
  other arithmetic  14.5 us (5%)
    psum x1, waiting for transfers between devices, local(): lax.psum(conv_weights(first_down, padded_in, fine_shape), ('space', 'filt'))  120 us
    ppermute x8, starting transfers between devices, extended(): lax.ppermute(tail, axis, [(i, (i + 1) % count) for i in range(ends)])  31.4 us
    unnamed x237, local copies, waits for them, and re-layouts  25.8 us
    reshape x58, local copies, waits for them, and re-layouts, window(): return section.reshape(padded.shape[0], extent_x * extent_y * extent_z)  17.6 us
    all_gather x1, blocking collectives, local(): whole_weight = lax.all_gather(second_weight, 'filt', axis=1, tiled=True)  15.2 us
    ppermute x8, starting transfers between devices, extended(): lax.ppermute(head, axis, [((i + 1) % count, i) for i in range(ends)])  10.8 us
    concatenate x10, other arithmetic, extended(): jnp.concatenate([lax.ppermute(tail, axis, [(i, (i + 1) % count) for i in...  9.21 us
    rev x27, local copies, waits for them, and re-layouts, conv_transpose(): tap_block = weight[24 - tap_base:27 - tap_base][::-1]  6.46 us
  transfers between devices with their start and end apart: 19, of which 6 were waited for; matrix products, arithmetic and copies ran while one was open for 27% of the time, Pallas kernels for 0%

commit v1 on v0

--- a/solution.py
+++ b/solution.py
@@ -152,7 +152,8 @@
     hidden_grad = spread_cells(pool_grad.reshape((channels,) + brick_shape))
     first_down = (hidden_grad.reshape(channels, -1) * silu_slope(first_pre)).astype(jnp.bfloat16)
     first_grad = (
-        lax.psum(conv_weights(first_down, padded_in, fine_shape), ("space", "filt")) * fine_scale
+        lax.psum(lax.psum(conv_weights(first_down, padded_in, fine_shape), "filt"), "space")
+        * fine_scale
     )
     padded_back = pad_depth(
         extended(first_down.reshape((channels,) + fine_shape), (("space", 1), ("filt", 2)), 1)

time: 318 us -> 456 us (1.43)
  waiting for transfers between devices: 131 us -> 258 us
    psum x1 -> x3, waiting for transfers between devices: 120 us -> 247 us  [the longest x1 137 us: local(): lax.psum(conv_weights(down_grad, padded_pool, brick_shape), ('space', 'fi...]
    unnamed x237 -> x221, local copies, waits for them, and re-layouts: 25.8 us -> 24.8 us
  transfers between devices with their start and end apart: 19 -> 21, of which waited for: 6 -> 7; matrix products, arithmetic and copies ran while one was open for 27% -> 23% of each run, Pallas kernels for 0% -> 0%
where the time goes in v1:
time: 456 us; the launch traced here: 455 us
  waiting for transfers between devices  258 us (57%)
  local copies, waits for them, and re-layouts  78.3 us (17%)
  starting transfers between devices  50.5 us (11%)
  other arithmetic  18.1 us (4%)
  matrix products  18 us (4%)
  between operations  16 us (4%)
  blocking collectives  15.2 us (3%)
    psum x1, waiting for transfers between devices, local(): lax.psum(conv_weights(down_grad, padded_pool, brick_shape), ('space', 'fi...  137 us
    psum x1, waiting for transfers between devices, local(): lax.psum(lax.psum(conv_weights(first_down, padded_in, fine_shape), 'filt'...  94.5 us
    ppermute x8, starting transfers between devices, extended(): lax.ppermute(tail, axis, [(i, (i + 1) % count) for i in range(ends)])  31.5 us
    unnamed x221, local copies, waits for them, and re-layouts  24.8 us
    reshape x58, local copies, waits for them, and re-layouts, window(): return section.reshape(padded.shape[0], extent_x * extent_y * extent_z)  18.2 us
    all_gather x1, blocking collectives, local(): whole_weight = lax.all_gather(second_weight, 'filt', axis=1, tiled=True)  15.2 us
    psum x1, waiting for transfers between devices, local(): lax.psum(conv_weights(first_down, padded_in, fine_shape), 'filt')  15.1 us
    concatenate x10, other arithmetic, extended(): jnp.concatenate([lax.ppermute(tail, axis, [(i, (i + 1) % count) for i in...  10.7 us
  transfers between devices with their start and end apart: 21, of which 7 were waited for; matrix products, arithmetic and copies ran while one was open for 23% of the time, Pallas kernels for 0%

profile of v1, /device:TPU:0, one launch (start us, length us, event | category | flops | bytes accessed | tf_op | source)
XLA Modules:
  0.0 454.6 jit_solution(16171870684719389689)
XLA Ops:
  7.2 1.4 copy.107
  8.5 4.2 all-to-all-start.1
  12.8 1.0 fusion.162
  13.7 1.3 collective-permute-start.1
  15.0 3.0 collective-permute-start
  18.1 1.3 copy.96
  19.4 15.2 %all_gather.3 = bf16[27,128,64]{2,0,1:T(8,128)(2,1)S(1)} all-gather(bf16[27,64,64]{2,0,1:T(8,128)(2,1)S(1)} %copy.96), channel_id=1, replica_groups=mesh['space'=16,'filt'=2] {'filt'}, dimensions={1}, use_global_device_ids=true | all-gather | bytes 663552 | tf_op jit(solution)/shard_map/all_gather | solution.py:124
  34.6 1.3 fusion.155
  36.4 1.2 fusion.160
  37.6 4.2 collective-permute-start.2
  41.8 1.5 collective-permute-start.3
  43.3 0.9 fusion.158
  45.5 1.8 copy.153
  47.3 1.0 copy.152
  48.3 1.6 copy.151
  49.9 1.6 copy.150
  51.5 1.6 copy.149
  56.0 1.4 rev.98
  70.2 1.7 pad_maximum_fusion.9
  75.6 2.4 select_maximum_fusion.2
  78.0 2.9 fusion.157
  89.7 1.1 constant_dynamic-update-slice_fusion.29
  90.9 1.2 fusion.163
  95.2 0.9 multiply_convert_fusion.1
  96.6 1.3 collective-permute-start.5
  97.9 3.0 collective-permute-start.4
  101.8 1.3 collective-permute-start.7
  103.1 4.8 %collective-permute-start.6 = (bf16[64,3,1,128]{3,0,2,1:T(8,128)(2,1)S(1)}, bf16[64,3,1,128]{3,0,2,1:T(8,128)(2,1)S(1)}, u32[]{:S(2)}, u32[]{:S(2)}) collective-permute-start(bf16[64,3,1,128]{3,0,2,1:T(8,128)(2,1)S(1)} %pad_maximum_fusion.18), channel_id=1, source_target_pairs={{0,1},{2,3},{4,5},{6,7},{8,9},{10,11},{12,13},{14,15},{16,17},{18,... | collective-permute-start | bytes 147464 | tf_op jit(solution)/shard_map/ppermute | solution.py:15
  107.9 1.5 collective-permute-done.6
  111.6 1.3 collective-permute-start.9
  112.9 3.9 collective-permute-start.8
  122.4 3.9 all-to-all-start
  126.9 1.0 copy.126
  127.9 1.7 copy.125
  129.6 1.7 copy.124
  131.3 1.7 copy.123
  133.0 0.9 bitcast_dynamic-update-slice_fusion.8
  134.0 0.9 bitcast_dynamic-update-slice_fusion.7
  134.9 0.9 bitcast_dynamic-update-slice_fusion.6
  136.0 1.2 copy-done
  138.0 1.3 collective-permute-start.11
  139.3 4.6 %collective-permute-start.10 = (bf16[128,3,1,128]{0,3,2,1:T(8,128)(2,1)S(1)}, bf16[128,3,1,128]{0,3,2,1:T(8,128)(2,1)S(1)}, u32[]{:S(2)}, u32[]{:S(2)}) collective-permute-start(bf16[128,3,1,128]{0,3,2,1:T(8,128)(2,1)S(1)} %pad_maximum_fusion.17), channel_id=1, source_target_pairs={{0,1},{2,3},{4,5},{6,7},{8,9},{10,11},{12,13},{14,15},{16,17},{18,... | collective-permute-start | bytes 294920 | tf_op jit(solution)/shard_map/ppermute | solution.py:15
  144.0 0.8 copy.131
  144.8 1.2 collective-permute-done.10
  147.3 5.5 %while.14 = (s32[]{:T(128)}, f32[64,128]{1,0:T(8,128)}, bf16[27,128,64]{2,1,0:T(8,128)(2,1)S(1)}, bf16[128,3,3,130]{3,0,2,1:T(8,128)(2,1)S(1)}, s32[]{:T(128)}, ...) while((s32[]{:T(128)}, f32[64,128]{1,0:T(8,128)}, ...), condition=%wide.region_2.3_spmd.clone, body=%wide.region_1.2_spmd.clone.sunk | while | flops 29736976 | bytes 3318213 | solution.py:149
  152.8 0.8 broadcast_multiply_fusion.1
  154.0 1.1 multiply_convert_fusion
  157.7 1.3 collective-permute-start.13
  159.0 3.9 collective-permute-start.12
  163.1 0.9 copy-done.12
  164.9 4.0 collective-permute-start.14
  169.0 1.3 collective-permute-start.15
  172.9 1.6 collective-permute-done.14
  174.6 7.1 %collective-permute-done.15 = bf16[64,4,1,256]{3,2,1,0:T(2,128)(2,1)S(1)} collective-permute-done((bf16[64,4,1,256]{3,2,1,0:T(2,128)(2,1)S(1)}, bf16[64,4,1,256]{3,2,1,0:T(2,128)(2,1)S(1)}, u32[]{:S(2)}, u32[]{:S(2)}) %collective-permute-start.15) | collective-permute-done | bytes 131104 | tf_op jit(solution)/shard_map/ppermute | solution.py:17
  181.7 1.7 pad_maximum_fusion.1
  185.2 2.4 select_maximum_fusion
  187.6 2.9 fusion.156
  192.8 1.0 convolution_add_fusion.15
  195.6 15.1 %all-reduce.8.cloned.1.call-done = f32[27,64,64]{1,2,0:T(8,128)} async-done(((f32[27,64,64]{1,2,0:T(8,128)}), f32[27,64,64]{1,2,0:T(8,128)}) %all-reduce.8.cloned.1.call-update) | async-done | bytes 442384 | tf_op jit(solution)/shard_map/psum | solution.py:155
  211.7 137.2 %all-reduce.12.cloned.1.call-done = f32[27,128,64]{2,1,0:T(8,128)} async-done(((f32[27,128,64]{2,1,0:T(8,128)}), f32[27,128,64]{2,1,0:T(8,128)}) %all-reduce.12.cloned.1.call-update) | async-done | bytes 884752 | tf_op jit(solution)/shard_map/psum | solution.py:134
  348.8 2.2 dynamic-slice_multiply_fusion
  351.0 94.5 %all-reduce.10.cloned.1.call-done = f32[27,64,64]{1,2,0:T(8,128)} async-done(((f32[27,64,64]{1,2,0:T(8,128)}), f32[27,64,64]{1,2,0:T(8,128)}) %all-reduce.10.cloned.1.call-update) | async-done | bytes 442384 | tf_op jit(solution)/shard_map/psum | solution.py:155
  445.5 1.3 broadcast_multiply_fusion
  446.8 1.2 copy.133
  (433 shorter events, 61.9 us)
Async XLA Ops:
  8.5 92.4 %all-to-all-start.1 = ((bf16[64,1,2,128]{3,0,1,2:T(8,128)(2,1)}), bf16[64,1,2,128]{3,0,1,2:T(8,128)(2,1)}, u32[]{:S(2)}, u32[]{:S(2)}) async-start(bf16[64,1,2,128]{3,0,1,2:T(8,128)(2,1)} %copy.107), calls=%async_computation.1 | async-start | bytes 65536 | tf_op jit(solution)/shard_map/all_to_all | solution.py:130
  13.7 22.2 %collective-permute-start.1 = (bf16[64,1,2,256]{3,2,1,0:T(2,128)(2,1)S(1)}, bf16[64,1,2,256]{3,2,1,0:T(2,128)(2,1)S(1)}, u32[]{:S(2)}, u32[]{:S(2)}) collective-permute-start(bf16[64,1,2,256]{3,2,1,0:T(2,128)(2,1)S(1)} %get-tuple-element.274), channel_id=1, source_target_pairs={{2,0},{4,2},{6,4},{8,6},{10,8},{12,10},{14,12},{16,14},{18,16},{20... | collective-permute-start | bytes 196616 | tf_op jit(solution)/shard_map/ppermute | solution.py:17
  15.0 20.9 %collective-permute-start = (bf16[64,1,2,256]{3,2,1,0:T(2,128)(2,1)S(1)}, bf16[64,1,2,256]{3,2,1,0:T(2,128)(2,1)S(1)}, u32[]{:S(2)}, u32[]{:S(2)}) collective-permute-start(bf16[64,1,2,256]{3,2,1,0:T(2,128)(2,1)S(1)} %get-tuple-element.275), channel_id=1, source_target_pairs={{0,2},{2,4},{4,6},{6,8},{8,10},{10,12},{12,14},{14,16},{16,18},{18... | collective-permute-start | bytes 196616 | tf_op jit(solution)/shard_map/ppermute | solution.py:15
  19.4 16.6 %copy-start.9 = (bf16[64,2,2,256]{3,2,1,0:T(2,128)(2,1)S(1)}, bf16[64,2,2,256]{3,2,1,0:T(2,128)(2,1)}, u32[]{:S(2)}) copy-start(bf16[64,2,2,256]{3,2,1,0:T(2,128)(2,1)} %param.6) | copy-start | bytes 393220
  34.6 8.6 %copy-start.33 = (bf16[27,64,64]{2,1,0:T(8,128)(2,1)S(1)}, bf16[27,64,64]{2,1,0:T(8,128)(2,1)}, u32[]{:S(2)}) copy-start(bf16[27,64,64]{2,1,0:T(8,128)(2,1)} %param.7) | copy-start | bytes 663556
  37.6 32.6 %collective-permute-start.2 = (bf16[64,4,1,256]{3,2,1,0:T(2,128)(2,1)}, bf16[64,4,1,256]{3,2,1,0:T(2,128)(2,1)S(1)}, u32[]{:S(2)}, u32[]{:S(2)}) collective-permute-start(bf16[64,4,1,256]{3,2,1,0:T(2,128)(2,1)} %get-tuple-element.264), channel_id=1, source_target_pairs={{0,1},{2,3},{4,5},{6,7},{8,9},{10,11},{12,13},{14,15},{16,17},{18,... | collective-permute-start | bytes 393224 | tf_op jit(solution)/shard_map/ppermute | solution.py:15
  41.8 28.4 %collective-permute-start.3 = (bf16[64,4,1,256]{3,2,1,0:T(2,128)(2,1)}, bf16[64,4,1,256]{3,2,1,0:T(2,128)(2,1)S(1)}, u32[]{:S(2)}, u32[]{:S(2)}) collective-permute-start(bf16[64,4,1,256]{3,2,1,0:T(2,128)(2,1)} %get-tuple-element.265), channel_id=1, source_target_pairs={{1,0},{3,2},{5,4},{7,6},{9,8},{11,10},{13,12},{15,14},{17,16},{19,... | collective-permute-start | bytes 393224 | tf_op jit(solution)/shard_map/ppermute | solution.py:17
  45.3 12.1 %copy-start.63 = (bf16[64,3,64]{2,0,1:T(8,128)(2,1)S(1)}, bf16[64,3,64]{2,0,1:T(8,128)(2,1)}, u32[]{:S(2)}) copy-start(bf16[64,3,64]{2,0,1:T(8,128)(2,1)} %get-tuple-element.221) | copy-start | bytes 73732
  45.3 12.8 %copy-start.62 = (bf16[64,3,64]{2,0,1:T(8,128)(2,1)S(1)}, bf16[64,3,64]{2,0,1:T(8,128)(2,1)}, u32[]{:S(2)}) copy-start(bf16[64,3,64]{2,0,1:T(8,128)(2,1)} %get-tuple-element.222) | copy-start | bytes 73732
  45.3 13.5 %copy-start.61 = (bf16[64,3,64]{2,0,1:T(8,128)(2,1)S(1)}, bf16[64,3,64]{2,0,1:T(8,128)(2,1)}, u32[]{:S(2)}) copy-start(bf16[64,3,64]{2,0,1:T(8,128)(2,1)} %get-tuple-element.223) | copy-start | bytes 73732
  45.3 14.3 %copy-start.60 = (bf16[64,3,64]{2,0,1:T(8,128)(2,1)S(1)}, bf16[64,3,64]{2,0,1:T(8,128)(2,1)}, u32[]{:S(2)}) copy-start(bf16[64,3,64]{2,0,1:T(8,128)(2,1)} %get-tuple-element.224) | copy-start | bytes 73732
  45.3 15.0 %copy-start.59 = (bf16[64,3,64]{2,0,1:T(8,128)(2,1)S(1)}, bf16[64,3,64]{2,0,1:T(8,128)(2,1)}, u32[]{:S(2)}) copy-start(bf16[64,3,64]{2,0,1:T(8,128)(2,1)} %get-tuple-element.225) | copy-start | bytes 73732
  45.4 15.7 %copy-start.58 = (bf16[64,3,64]{2,0,1:T(8,128)(2,1)S(1)}, bf16[64,3,64]{2,0,1:T(8,128)(2,1)}, u32[]{:S(2)}) copy-start(bf16[64,3,64]{2,0,1:T(8,128)(2,1)} %get-tuple-element.226) | copy-start | bytes 73732
  45.4 16.4 %copy-start.57 = (bf16[64,3,64]{2,0,1:T(8,128)(2,1)S(1)}, bf16[64,3,64]{2,0,1:T(8,128)(2,1)}, u32[]{:S(2)}) copy-start(bf16[64,3,64]{2,0,1:T(8,128)(2,1)} %get-tuple-element.227) | copy-start | bytes 73732
  45.4 17.1 %copy-start.56 = (bf16[64,3,64]{2,0,1:T(8,128)(2,1)S(1)}, bf16[64,3,64]{2,0,1:T(8,128)(2,1)}, u32[]{:S(2)}) copy-start(bf16[64,3,64]{2,0,1:T(8,128)(2,1)} %get-tuple-element.228) | copy-start | bytes 73732
  45.4 17.8 %copy-start.55 = (bf16[64,3,64]{2,0,1:T(8,128)(2,1)S(1)}, bf16[64,3,64]{2,0,1:T(8,128)(2,1)}, u32[]{:S(2)}) copy-start(bf16[64,3,64]{2,0,1:T(8,128)(2,1)} %get-tuple-element.229) | copy-start | bytes 73732
  45.4 18.5 %copy-start.54 = (bf16[3,64,64]{2,1,0:T(8,128)(2,1)S(1)}, bf16[3,64,64]{2,1,0:T(8,128)(2,1)}, u32[]{:S(2)}) copy-start(bf16[3,64,64]{2,1,0:T(8,128)(2,1)} %get-tuple-element.230) | copy-start | bytes 73732
  45.4 19.1 %copy-start.53 = (bf16[3,64,64]{2,1,0:T(8,128)(2,1)S(1)}, bf16[3,64,64]{2,1,0:T(8,128)(2,1)}, u32[]{:S(2)}) copy-start(bf16[3,64,64]{2,1,0:T(8,128)(2,1)} %get-tuple-element.231) | copy-start | bytes 73732
  45.4 19.7 %copy-start.52 = (bf16[3,64,64]{2,1,0:T(8,128)(2,1)S(1)}, bf16[3,64,64]{2,1,0:T(8,128)(2,1)}, u32[]{:S(2)}) copy-start(bf16[3,64,64]{2,1,0:T(8,128)(2,1)} %get-tuple-element.232) | copy-start | bytes 73732
  45.4 20.3 %copy-start.51 = (bf16[3,64,64]{2,1,0:T(8,128)(2,1)S(1)}, bf16[3,64,64]{2,1,0:T(8,128)(2,1)}, u32[]{:S(2)}) copy-start(bf16[3,64,64]{2,1,0:T(8,128)(2,1)} %get-tuple-element.233) | copy-start | bytes 73732
  45.4 20.9 %copy-start.50 = (bf16[3,64,64]{2,1,0:T(8,128)(2,1)S(1)}, bf16[3,64,64]{2,1,0:T(8,128)(2,1)}, u32[]{:S(2)}) copy-start(bf16[3,64,64]{2,1,0:T(8,128)(2,1)} %get-tuple-element.234) | copy-start | bytes 73732
  45.4 21.5 %copy-start.49 = (bf16[3,64,64]{2,1,0:T(8,128)(2,1)S(1)}, bf16[3,64,64]{2,1,0:T(8,128)(2,1)}, u32[]{:S(2)}) copy-start(bf16[3,64,64]{2,1,0:T(8,128)(2,1)} %get-tuple-element.235) | copy-start | bytes 73732
  45.5 22.1 %copy-start.48 = (bf16[3,64,64]{2,1,0:T(8,128)(2,1)S(1)}, bf16[3,64,64]{2,1,0:T(8,128)(2,1)}, u32[]{:S(2)}) copy-start(bf16[3,64,64]{2,1,0:T(8,128)(2,1)} %get-tuple-element.236) | copy-start | bytes 73732
  45.5 22.8 %copy-start.47 = (bf16[3,64,64]{2,1,0:T(8,128)(2,1)S(1)}, bf16[3,64,64]{2,1,0:T(8,128)(2,1)}, u32[]{:S(2)}) copy-start(bf16[3,64,64]{2,1,0:T(8,128)(2,1)} %get-tuple-element.237) | copy-start | bytes 73732
  87.8 3.0 copy-start.24
  89.5 2.7 copy-start.31
  89.5 2.7 copy-start.28
  89.6 2.7 copy-start.22
  89.6 2.8 copy-start.27
  89.6 2.7 copy-start.16
  89.7 2.8 copy-start.26
  89.7 2.8 copy-start.17
  95.2 14.5 %copy-start.83 = (bf16[3,128,64]{1,2,0:T(8,128)(2,1)S(1)}, bf16[3,128,64]{1,2,0:T(8,128)(2,1)}, u32[]{:S(2)}) copy-start(bf16[3,128,64]{1,2,0:T(8,128)(2,1)} %copy.145) | copy-start | bytes 147460
  95.2 14.7 %copy-start.39 = (bf16[3,128,64]{1,2,0:T(8,128)(2,1)S(1)}, bf16[3,128,64]{1,2,0:T(8,128)(2,1)}, u32[]{:S(2)}) copy-start(bf16[3,128,64]{1,2,0:T(8,128)(2,1)} %copy.146) | copy-start | bytes 147460
  95.2 15.0 %copy-start.38 = (bf16[3,128,64]{1,2,0:T(8,128)(2,1)S(1)}, bf16[3,128,64]{1,2,0:T(8,128)(2,1)}, u32[]{:S(2)}) copy-start(bf16[3,128,64]{1,2,0:T(8,128)(2,1)} %copy.147) | copy-start | bytes 147460
  96.2 14.2 %copy-start.37 = (bf16[3,128,64]{1,2,0:T(8,128)(2,1)S(1)}, bf16[3,128,64]{1,2,0:T(8,128)(2,1)}, u32[]{:S(2)}) copy-start(bf16[3,128,64]{1,2,0:T(8,128)(2,1)} %copy.148) | copy-start | bytes 147460
  96.2 14.4 %copy-start.36 = (bf16[3,128,64]{1,2,0:T(8,128)(2,1)S(1)}, bf16[3,128,64]{1,2,0:T(8,128)(2,1)}, u32[]{:S(2)}) copy-start(bf16[3,128,64]{1,2,0:T(8,128)(2,1)} %copy.149) | copy-start | bytes 147460
  96.2 14.6 %copy-start.35 = (bf16[3,128,64]{1,2,0:T(8,128)(2,1)S(1)}, bf16[3,128,64]{1,2,0:T(8,128)(2,1)}, u32[]{:S(2)}) copy-start(bf16[3,128,64]{1,2,0:T(8,128)(2,1)} %copy.150) | copy-start | bytes 147460
  96.2 14.8 %copy-start.34 = (bf16[3,128,64]{1,2,0:T(8,128)(2,1)S(1)}, bf16[3,128,64]{1,2,0:T(8,128)(2,1)}, u32[]{:S(2)}) copy-start(bf16[3,128,64]{1,2,0:T(8,128)(2,1)} %copy.151) | copy-start | bytes 147460
  96.5 14.8 %copy-start.82 = (bf16[3,128,64]{1,2,0:T(8,128)(2,1)S(1)}, bf16[3,128,64]{1,2,0:T(8,128)(2,1)}, u32[]{:S(2)}) copy-start(bf16[3,128,64]{1,2,0:T(8,128)(2,1)} %copy.153) | copy-start | bytes 147460
  96.6 5.2 %collective-permute-start.5 = (bf16[64,1,1,128]{3,0,2,1:T(8,128)(2,1)S(1)}, bf16[64,1,1,128]{3,0,2,1:T(8,128)(2,1)S(1)}, u32[]{:S(2)}, u32[]{:S(2)}) collective-permute-start(bf16[64,1,1,128]{3,0,2,1:T(8,128)(2,1)S(1)} %fusion.245), channel_id=1, source_target_pairs={{2,0},{4,2},{6,4},{8,6},{10,8},{12,10},{14,12},{16,14},{18,16},{20... | collective-permute-start | bytes 49160 | tf_op jit(solution)/shard_map/ppermute | solution.py:17
  97.9 3.9 collective-permute-start.4
  101.8 6.1 %collective-permute-start.7 = (bf16[64,3,1,128]{3,0,2,1:T(8,128)(2,1)S(1)}, bf16[64,3,1,128]{3,0,2,1:T(8,128)(2,1)S(1)}, u32[]{:S(2)}, u32[]{:S(2)}) collective-permute-start(bf16[64,3,1,128]{3,0,2,1:T(8,128)(2,1)S(1)} %pad_maximum_fusion.18), channel_id=1, source_target_pairs={{1,0},{3,2},{5,4},{7,6},{9,8},{11,10},{13,12},{15,14},{17,16},{19,... | collective-permute-start | bytes 147464 | tf_op jit(solution)/shard_map/ppermute | solution.py:17
  103.1 6.3 %collective-permute-start.6 = (bf16[64,3,1,128]{3,0,2,1:T(8,128)(2,1)S(1)}, bf16[64,3,1,128]{3,0,2,1:T(8,128)(2,1)S(1)}, u32[]{:S(2)}, u32[]{:S(2)}) collective-permute-start(bf16[64,3,1,128]{3,0,2,1:T(8,128)(2,1)S(1)} %pad_maximum_fusion.18), channel_id=1, source_target_pairs={{0,1},{2,3},{4,5},{6,7},{8,9},{10,11},{12,13},{14,15},{16,17},{18,... | collective-permute-start | bytes 147464 | tf_op jit(solution)/shard_map/ppermute | solution.py:15
  109.7 10.5 %copy-start.67 = (bf16[64,128]{1,0:T(8,128)(2,1)}, bf16[64,128]{1,0:T(8,128)(2,1)S(1)}, u32[]{:S(2)}) copy-start(bf16[64,128]{1,0:T(8,128)(2,1)S(1)} %get-tuple-element.238) | copy-start | bytes 49156
  109.7 10.5 %copy-start.69 = (bf16[64,128]{1,0:T(8,128)(2,1)}, bf16[64,128]{1,0:T(8,128)(2,1)S(1)}, u32[]{:S(2)}) copy-start(bf16[64,128]{1,0:T(8,128)(2,1)S(1)} %get-tuple-element.255) | copy-start | bytes 49156
  110.2 9.0 %copy-start.71 = (bf16[64,128]{1,0:T(8,128)(2,1)}, bf16[64,128]{1,0:T(8,128)(2,1)S(1)}, u32[]{:S(2)}) copy-start(bf16[64,128]{1,0:T(8,128)(2,1)S(1)} %get-tuple-element.278) | copy-start | bytes 49156
  111.6 24.4 %collective-permute-start.9 = (bf16[128,1,1,128]{0,3,2,1:T(8,128)(2,1)S(1)}, bf16[128,1,1,128]{0,3,2,1:T(8,128)(2,1)S(1)}, u32[]{:S(2)}, u32[]{:S(2)}) collective-permute-start(bf16[128,1,1,128]{0,3,2,1:T(8,128)(2,1)S(1)} %bitcast.408), channel_id=1, source_target_pairs={{2,0},{4,2},{6,4},{8,6},{10,8},{12,10},{14,12},{16,14},{18,16},{20... | collective-permute-start | bytes 98312 | tf_op jit(solution)/shard_map/ppermute | solution.py:17
  112.9 23.1 %collective-permute-start.8 = (bf16[128,1,1,128]{0,3,2,1:T(8,128)(2,1)S(1)}, bf16[128,1,1,128]{0,3,2,1:T(8,128)(2,1)}, u32[]{:S(2)}, u32[]{:S(2)}) collective-permute-start(bf16[128,1,1,128]{0,3,2,1:T(8,128)(2,1)S(1)} %bitcast.409), channel_id=1, source_target_pairs={{0,2},{2,4},{4,6},{6,8},{8,10},{10,12},{12,14},{14,16},{16,18},{18... | collective-permute-start | bytes 98312 | tf_op jit(solution)/shard_map/ppermute | solution.py:15
  122.4 48.9 %all-to-all-start = ((bf16[2,2,4096]{2,1,0:T(2,128)(2,1)}), bf16[2,2,4096]{2,1,0:T(2,128)(2,1)}, u32[]{:S(2)}, u32[]{:S(2)}) async-start(bf16[2,2,4096]{2,1,0:T(2,128)(2,1)} %reshape.942), calls=%async_computation | async-start | bytes 65536 | tf_op jit(solution)/shard_map/all_to_all | solution.py:129
  126.3 84.4 %all-reduce.8.cloned.1.call-start = ((), (), s32[]{:S(2)}) async-start(), calls=%async_computation.2 | async-start | bytes 1769472 | tf_op jit(solution)/shard_map/psum | solution.py:155
  131.3 12.5 %copy-start.68 = (bf16[64,128]{1,0:T(8,128)(2,1)S(1)}, bf16[64,128]{1,0:T(8,128)(2,1)}, u32[]{:S(2)}) copy-start(bf16[64,128]{1,0:T(8,128)(2,1)} %copy-done.67) | copy-start | bytes 49156
  131.3 12.5 %copy-start.70 = (bf16[64,128]{1,0:T(8,128)(2,1)S(1)}, bf16[64,128]{1,0:T(8,128)(2,1)}, u32[]{:S(2)}) copy-start(bf16[64,128]{1,0:T(8,128)(2,1)} %copy-done.69) | copy-start | bytes 49156
  131.3 12.5 %copy-start.72 = (bf16[64,128]{1,0:T(8,128)(2,1)S(1)}, bf16[64,128]{1,0:T(8,128)(2,1)}, u32[]{:S(2)}) copy-start(bf16[64,128]{1,0:T(8,128)(2,1)} %copy-done.71) | copy-start | bytes 49156
  138.0 6.9 %collective-permute-start.11 = (bf16[128,3,1,128]{0,3,2,1:T(8,128)(2,1)S(1)}, bf16[128,3,1,128]{0,3,2,1:T(8,128)(2,1)S(1)}, u32[]{:S(2)}, u32[]{:S(2)}) collective-permute-start(bf16[128,3,1,128]{0,3,2,1:T(8,128)(2,1)S(1)} %pad_maximum_fusion.17), channel_id=1, source_target_pairs={{1,0},{3,2},{5,4},{7,6},{9,8},{11,10},{13,12},{15,14},{17,16},{19,... | collective-permute-start | bytes 294920 | tf_op jit(solution)/shard_map/ppermute | solution.py:17
  139.3 6.8 %collective-permute-start.10 = (bf16[128,3,1,128]{0,3,2,1:T(8,128)(2,1)S(1)}, bf16[128,3,1,128]{0,3,2,1:T(8,128)(2,1)S(1)}, u32[]{:S(2)}, u32[]{:S(2)}) collective-permute-start(bf16[128,3,1,128]{0,3,2,1:T(8,128)(2,1)S(1)} %pad_maximum_fusion.17), channel_id=1, source_target_pairs={{0,1},{2,3},{4,5},{6,7},{8,9},{10,11},{12,13},{14,15},{16,17},{18,... | collective-permute-start | bytes 294920 | tf_op jit(solution)/shard_map/ppermute | solution.py:15
  157.7 6.4 %collective-permute-start.13 = (bf16[64,1,2,256]{3,2,1,0:T(2,128)(2,1)S(1)}, bf16[64,1,2,256]{3,2,1,0:T(2,128)(2,1)S(1)}, u32[]{:S(2)}, u32[]{:S(2)}) collective-permute-start(bf16[64,1,2,256]{3,2,1,0:T(2,128)(2,1)S(1)} %get-tuple-element.269), channel_id=1, source_target_pairs={{2,0},{4,2},{6,4},{8,6},{10,8},{12,10},{14,12},{16,14},{18,16},{20... | collective-permute-start | bytes 196616 | tf_op jit(solution)/shard_map/ppermute | solution.py:17
  159.0 5.1 %collective-permute-start.12 = (bf16[64,1,2,256]{3,2,1,0:T(2,128)(2,1)S(1)}, bf16[64,1,2,256]{3,2,1,0:T(2,128)(2,1)S(1)}, u32[]{:S(2)}, u32[]{:S(2)}) collective-permute-start(bf16[64,1,2,256]{3,2,1,0:T(2,128)(2,1)S(1)} %get-tuple-element.270), channel_id=1, source_target_pairs={{0,2},{2,4},{4,6},{6,8},{8,10},{10,12},{12,14},{14,16},{16,18},{18... | collective-permute-start | bytes 196616 | tf_op jit(solution)/shard_map/ppermute | solution.py:15
  163.0 7.3 %copy-start.13 = (f32[128,3,64]{2,0,1:T(8,128)S(1)}, f32[128,3,64]{2,0,1:T(8,128)}, u32[]{:S(2)}) copy-start(f32[128,3,64]{2,0,1:T(8,128)} %copy.131) | copy-start | bytes 294916
  164.0 184.8 %all-reduce.12.cloned.1.call-start = ((), (), s32[]{:S(2)}) async-start(), calls=%async_computation.4 | async-start | bytes 3538944 | tf_op jit(solution)/shard_map/psum | solution.py:134
  164.9 9.6 %collective-permute-start.14 = (bf16[64,4,1,256]{3,2,1,0:T(2,128)(2,1)S(1)}, bf16[64,4,1,256]{3,2,1,0:T(2,128)(2,1)S(1)}, u32[]{:S(2)}, u32[]{:S(2)}) collective-permute-start(bf16[64,4,1,256]{3,2,1,0:T(2,128)(2,1)S(1)} %get-tuple-element.259), channel_id=1, source_target_pairs={{0,1},{2,3},{4,5},{6,7},{8,9},{10,11},{12,13},{14,15},{16,17},{18,... | collective-permute-start | bytes 393224 | tf_op jit(solution)/shard_map/ppermute | solution.py:15
  169.0 12.7 %collective-permute-start.15 = (bf16[64,4,1,256]{3,2,1,0:T(2,128)(2,1)S(1)}, bf16[64,4,1,256]{3,2,1,0:T(2,128)(2,1)S(1)}, u32[]{:S(2)}, u32[]{:S(2)}) collective-permute-start(bf16[64,4,1,256]{3,2,1,0:T(2,128)(2,1)S(1)} %get-tuple-element.260), channel_id=1, source_target_pairs={{1,0},{3,2},{5,4},{7,6},{9,8},{11,10},{13,12},{15,14},{17,16},{19,... | collective-permute-start | bytes 393224 | tf_op jit(solution)/shard_map/ppermute | solution.py:17
  171.0 274.5 %all-reduce.10.cloned.1.call-start = ((), (), s32[]{:S(2)}) async-start(), calls=%async_computation.3 | async-start | bytes 1769472 | tf_op jit(solution)/shard_map/psum | solution.py:155
  195.1 15.6 %copy-start.73 = (bf16[3,64,64]{2,1,0:T(8,128)(2,1)S(1)}, bf16[3,64,64]{2,1,0:T(8,128)(2,1)}, u32[]{:S(2)}) copy-start(bf16[3,64,64]{2,1,0:T(8,128)(2,1)} %rev.98) | copy-start | bytes 73732
  (44 other events, 66.6 us)
Sparse Core Ops, SparseCore 0:
  164.1 46.4 all-reduce.7
  216.0 132.7 all-reduce.11
  352.3 93.2 all-reduce.9
